TPU v7x, 32 devices: a whole 2x2x4 slice. The times are simulated.
32 devices in a mesh: grp: 2 (over y), row: 16 (over z, x, core).
Axes of the slice: x: 2, y: 2, z: 4, core: 2. Of those that a mesh axis runs over, the one named last changes fastest.
Arguments:
- features: float32 [128, 32, 512], P(('grp', 'row')), parts along dimension 0, may hold values from -6 to 6
- cotangent: float32 [128, 32, 512], P(('grp', 'row')), parts along dimension 0, may hold values from -8 to 8
- kernel: float32 [7, 7, 512], replicated, may hold values from -0.875 to 0.875
- norm_gain: float32 [512], replicated, may hold values from 0.1 to 1.9
- norm_bias: float32 [512], replicated, may hold values from -3 to 3
- in_weight: float32 [512, 2048], P('row'), may hold values from -0.25 to 0.25
- in_bias: float32 [2048], replicated, may hold values from -3 to 3
- out_weight: float32 [512, 2048], P('row'), may hold values from -0.125 to 0.125
- layer_scale: float32 [512], replicated, may hold values from 0.3 to 1.5
Outputs:
- output: float32 [128, 32, 512], P(('grp', 'row')), parts along dimension 0
- input_grad: float32 [128, 32, 512], P(('grp', 'row')), parts along dimension 0
- in_weight_grad: float32 [1024, 2048], P(('grp', 'row')), parts along dimension 0
- out_weight_grad: float32 [1024, 2048], P(('grp', 'row')), parts along dimension 0
- kernel_grad: float32 [14, 7, 512], P('grp'), parts along dimension 0
- gain_grad: float32 [1024], P('grp'), parts along dimension 0
- bias_grad: float32 [1024], P('grp'), parts along dimension 0
- in_bias_grad: float32 [4096], P('grp'), parts along dimension 0
- scale_grad: float32 [1024], P('grp'), parts along dimension 0
There are 2 independent parts, one for each index of `grp`. A program takes and returns all parts, laid end to end along the dimension named above; an argument that names none is the same for every part. Nothing has to cross between parts.
All inputs are finite; a program needn't handle non-finite values.
Results may differ from a plain program's by a relative error of at most 0.0071.
Values may be sent and summed in bfloat16 or wider, within the bound.
A program may use at most 64 MiB of HBM per device.

v0:
```python
import math

import jax
import jax.numpy as jnp
from jax import lax
from jax.sharding import PartitionSpec as P


def extended(block, sides, width):
    for axis, dim in sides:
        count = lax.axis_size(axis)
        forward = [(i, i + 1) for i in range(count - 1)]
        backward = [(target, source) for source, target in forward]
        low = lax.ppermute(
            lax.slice_in_dim(block, block.shape[dim] - width, None, axis=dim), axis, forward
        )
        high = lax.ppermute(lax.slice_in_dim(block, 0, width, axis=dim), axis, backward)
        block = jnp.concatenate([low, block, high], axis=dim)
    return block


def conv_taps(padded, kernel, row_count, col_count):
    running = jnp.zeros((row_count, col_count, padded.shape[2]), jnp.float32)
    for tap_row in range(7):
        for tap_col in range(7):
            running = (
                running
                + padded[tap_row : tap_row + row_count, tap_col : tap_col + col_count]
                * kernel[tap_row, tap_col]
            )
    return running


def contract_last(left, right):
    return lax.dot_general(
        left, right, (((1,), (1,)), ((), ())), preferred_element_type=jnp.float32
    )


def contract_first(left, right):
    return lax.dot_general(
        left, right, (((0,), (0,)), ((), ())), preferred_element_type=jnp.float32
    )


def per_device(
    features, cotangent, kernel, norm_gain, norm_bias, in_weight, in_bias, out_weight, layer_scale
):
    row_count, col_count, channels = features.shape
    hidden_count = in_weight.shape[1]
    norm_scale = 1.0 / math.sqrt(row_count * col_count * lax.axis_size("row"))
    rimmed = extended(features, (("row", 0),), 3)
    padded = jnp.pad(rimmed, ((0, 0), (3, 3), (0, 0)))
    convolved = conv_taps(padded, kernel, row_count, col_count).reshape(-1, channels)
    average = jnp.mean(convolved, axis=1, keepdims=True)
    centred = convolved - average
    inv_std = lax.rsqrt(jnp.mean(centred * centred, axis=1, keepdims=True) + 1e-06)
    normed = centred * inv_std
    normed_out = (normed * norm_gain + norm_bias).astype(jnp.bfloat16)
    in_narrow = in_weight.astype(jnp.bfloat16)
    out_narrow = out_weight.astype(jnp.bfloat16)

    def fold_rows(left, piece):
        return jnp.dot(left, piece, preferred_element_type=jnp.float32)

    def map_rows(left, piece):
        return contract_last(left, piece)

    preact = fold_rows(normed_out, lax.all_gather(in_narrow, "row", axis=0, tiled=True)) + in_bias
    cdf_value = 0.5 * (1.0 + jax.scipy.special.erf(preact * 0.7071067811865476))
    activated = (preact * cdf_value).astype(jnp.bfloat16)
    mixed = map_rows(activated, lax.all_gather(out_narrow, "row", axis=0, tiled=True))
    flat_input = features.reshape(-1, channels)
    flat_cotan = cotangent.reshape(-1, channels)
    output = (flat_input + layer_scale * mixed).reshape(row_count, col_count, channels)
    scale_term = jnp.sum(flat_cotan * mixed, axis=0)
    branch_grad = (layer_scale * flat_cotan).astype(jnp.bfloat16)
    act_grad = fold_rows(branch_grad, lax.all_gather(out_narrow, "row", axis=0, tiled=True))
    gelu_slope = cdf_value + preact * jnp.exp(-0.5 * preact * preact) * 0.3989422804014327
    hidden_grad = act_grad * gelu_slope
    in_bias_term = jnp.sum(hidden_grad, axis=0)
    hidden_narrow = hidden_grad.astype(jnp.bfloat16)
    out_grad = map_rows(hidden_narrow, lax.all_gather(in_narrow, "row", axis=0, tiled=True))
    gain_term = jnp.sum(out_grad * normed, axis=0)
    bias_term = jnp.sum(out_grad, axis=0)
    normed_grad = out_grad * norm_gain
    conv_grad = inv_std * (
        normed_grad
        - jnp.mean(normed_grad, axis=1, keepdims=True)
        - normed * jnp.mean(normed_grad * normed, axis=1, keepdims=True)
    )
    grad_pairs = lax.psum_scatter(
        jnp.concatenate(
            [
                norm_scale * contract_first(normed_out, hidden_narrow),
                norm_scale * contract_first(branch_grad, activated),
            ],
            axis=1,
        ),
        "row",
        scatter_dimension=0,
        tiled=True,
    )
    in_weight_grad = grad_pairs[:, :hidden_count]
    out_weight_grad = grad_pairs[:, hidden_count:]
    conv_grid = conv_grad.reshape(row_count, col_count, channels)
    grad_rimmed = extended(conv_grid, (("row", 0),), 3)
    grad_padded = jnp.pad(grad_rimmed, ((0, 0), (3, 3), (0, 0)))
    input_grad = cotangent
    kernel_rows = []
    for tap_row in range(7):
        tap_list = []
        for tap_col in range(7):
            input_grad = (
                input_grad
                + kernel[tap_row, tap_col]
                * grad_padded[
                    6 - tap_row : 6 - tap_row + row_count, 6 - tap_col : 6 - tap_col + col_count
                ]
            )
            tap_list.append(
                jnp.sum(
                    padded[tap_row : tap_row + row_count, tap_col : tap_col + col_count]
                    * conv_grid,
                    axis=(0, 1),
                )
            )
        kernel_rows.append(jnp.stack(tap_list))
    kernel_term = norm_scale * jnp.stack(kernel_rows)
    small_sums = lax.psum(
        (
            kernel_term,
            norm_scale * gain_term,
            norm_scale * bias_term,
            norm_scale * in_bias_term,
            norm_scale * scale_term,
        ),
        "row",
    )
    return (
        output,
        input_grad,
        in_weight_grad,
        out_weight_grad,
        small_sums[0],
        small_sums[1],
        small_sums[2],
        small_sums[3],
        small_sums[4],
    )


def solution(mesh):
    return jax.shard_map(
        per_device,
        mesh=mesh,
        in_specs=(
            P(("grp", "row"), None, None),
            P(("grp", "row"), None, None),
            P(),
            P(),
            P(),
            P("row", None),
            P(),
            P("row", None),
            P(),
        ),
        out_specs=(
            P(("grp", "row"), None, None),
            P(("grp", "row"), None, None),
            P(("grp", "row"), None),
            P(("grp", "row"), None),
            P("grp", None, None),
            P("grp"),
            P("grp"),
            P("grp"),
            P("grp"),
        ),
        check_vma=False,
    )
```

profile of v0, /device:TPU:0, one launch (start us, length us, event | category | flops | bytes accessed | tf_op | source)
XLA Modules:
  0.0 309.9 jit_solution(13903080589390694371)
XLA Ops:
  7.2 1.7 convert_element_type.22
  9.0 1.6 convert_element_type.24
  11.7 2.4 collective-permute-start
  14.1 1.3 collective-permute-start.1
  15.4 1.2 fusion.74
  19.9 1.3 select_maximum_fusion.2
  21.2 2.0 fusion.70
  24.0 31.1 %all-gather.3.cloned.1.call-done = bf16[512,2048]{1,0:T(8,128)(2,1)} async-done(((bf16[32,2048]{1,0:T(8,128)(2,1)}), bf16[512,2048]{1,0:T(8,128)(2,1)}) %all-gather.3.cloned.1.call-update) | async-done | bytes 2097168 | tf_op jit(solution)/shard_map/all_gather | solution.py:69
  55.0 2.1 multiply_convert_fusion
  57.2 40.8 %all-gather.5.cloned.1.call-done = bf16[512,2048]{1,0:T(8,128)(2,1)} async-done(((bf16[32,2048]{1,0:T(8,128)(2,1)}), bf16[512,2048]{1,0:T(8,128)(2,1)}) %all-gather.5.cloned.1.call-update) | async-done | bytes 2097168 | tf_op jit(solution)/shard_map/all_gather | solution.py:72
  98.0 3.9 %fusion.65 = (f32[512]{0:T(512)}, bf16[128,512]{1,0:T(8,128)(2,1)S(1)}, f32[128,512]{1,0:T(8,128)}) fusion(f32[4,32,512]{2,1,0:T(8,128)S(1)} %copy-done.8, f32[512]{0:T(512)} %param.17, f32[4,32,512]{2,1,0:T(8,128)S(1)} %copy-done, bf16[128,2048]{1,0:T(8,128)(2,1)S(1)} %get-tuple-element.138, bf16[512,2048]{1,0:T(8,128)(2,1)} %all-gather.5.cloned.1.call-done), kind=kOutput, calls=%fused_computation.133 | convolution fusion | flops 268828160 | bytes 3543040 | tf_op jit(solution)/shard_map/dot_general | solution.py:35
  102.6 1.4 fusion.77
  104.7 3.8 %pad_maximum_fusion = f32[512,4096]{1,0:T(8,128)} fusion(f32[512,2048]{1,0:T(8,128)S(1)} %convolution_multiply_fusion, f32[512,2048]{1,0:T(8,128)S(1)} %convolution_multiply_fusion.1), kind=kLoop, calls=%fused_computation | loop fusion | flops 2097152 | bytes 16777216 | tf_op jit(solution)/shard_map/concatenate | solution.py:93
  108.6 1.5 copy-done.1
  110.1 2.7 multiply_reduce_fusion
  112.7 1.3 multiply_reduce_fusion.1
  114.1 2.2 collective-permute-start.2
  116.3 1.4 collective-permute-start.3
  120.0 62.8 %all-reduce.2 = (f32[512]{0:T(512)}, f32[512]{0:T(512)}, f32[2048]{0:T(1024)}, f32[512]{0:T(512)}) all-reduce(f32[512]{0:T(512)S(1)} %get-tuple-element.144, f32[512]{0:T(512)S(1)} %get-tuple-element.143, f32[2048]{0:T(1024)S(1)} %broadcast_multiply_fusion.1, ...), channel_id=1, replica_groups=mesh['grp'=2,'row'=16] {'row'}, use_global_device_ids=true, to_apply=%region_56.57 | all-reduce | flops 3584 | bytes 28672 | tf_op jit(solution)/shard_map/psum | solution.py:130
  183.2 2.6 fusion.17
  185.8 26.6 %reduce-scatter.2.cloned.1.call-done = f32[32,4096]{1,0:T(8,128)} async-done(((f32[512,4096]{1,0:T(8,128)}), f32[32,4096]{1,0:T(8,128)}) %reduce-scatter.2.cloned.1.call-update) | async-done | bytes 524304 | tf_op jit(solution)/shard_map/reduce_scatter | solution.py:92
  212.4 1.9 fusion.71
  214.2 87.5 %all-reduce.5.cloned.1.call-done = f32[7,7,512]{2,1,0:T(8,128)} async-done(((f32[7,7,512]{2,1,0:T(8,128)}), f32[7,7,512]{2,1,0:T(8,128)}) %all-reduce.5.cloned.1.call-update) | async-done | bytes 100368 | tf_op jit(solution)/shard_map/psum | solution.py:130
  301.8 1.6 copy.27
  (174 shorter events, 8.5 us)
Async XLA Ops:
  7.2 47.8 %all-gather.3.cloned.1.call-start = ((), (), s32[]{:S(2)}) async-start(), calls=%async_computation.1 | async-start | bytes 2228224 | tf_op jit(solution)/shard_map/all_gather | solution.py:69
  8.9 89.1 %all-gather.5.cloned.1.call-start = ((), (), s32[]{:S(2)}) async-start(), calls=%async_computation.2 | async-start | bytes 2228224 | tf_op jit(solution)/shard_map/all_gather | solution.py:72
  10.6 201.8 %reduce-scatter.2.cloned.1.call-start = ((), (), s32[]{:S(2)}) async-start(), calls=%async_computation.3 | async-start | bytes 8912896 | tf_op jit(solution)/shard_map/reduce_scatter | solution.py:92
  11.7 7.1 %collective-permute-start = (f32[3,32,512]{2,1,0:T(8,128)S(1)}, f32[3,32,512]{2,1,0:T(8,128)S(1)}, u32[]{:S(2)}, u32[]{:S(2)}) collective-permute-start(f32[3,32,512]{2,1,0:T(8,128)S(1)} %get-tuple-element.87), channel_id=1, source_target_pairs={{0,1},{1,2},{2,3},{3,4},{4,5},{5,6},{6,7},{7,8},{8,9},{9,10},{10,1... | collective-permute-start | bytes 589832 | tf_op jit(solution)/shard_map/ppermute | solution.py:14
  14.1 5.8 %collective-permute-start.1 = (f32[3,32,512]{2,1,0:T(8,128)S(1)}, f32[3,32,512]{2,1,0:T(8,128)S(1)}, u32[]{:S(2)}, u32[]{:S(2)}) collective-permute-start(f32[3,32,512]{2,1,0:T(8,128)S(1)} %get-tuple-element.88), channel_id=1, source_target_pairs={{1,0},{2,1},{3,2},{4,3},{5,4},{6,5},{7,6},{8,7},{9,8},{10,9},{11,1... | collective-permute-start | bytes 589832 | tf_op jit(solution)/shard_map/ppermute | solution.py:17
  23.4 74.5 %copy-start.8 = (f32[4,32,512]{2,1,0:T(8,128)S(1)}, f32[4,32,512]{2,1,0:T(8,128)}, u32[]{:S(2)}) copy-start(f32[4,32,512]{2,1,0:T(8,128)} %param.10) | copy-start | bytes 786436
  23.5 74.4 %copy-start.60 = (f32[128]{0:T(128)}, f32[128]{0:T(128)S(1)}, u32[]{:S(2)}) copy-start(f32[128]{0:T(128)S(1)} %div.15) | copy-start | bytes 1540
  23.8 74.2 %copy-start.61 = (f32[128]{0:T(128)}, f32[128]{0:T(128)S(1)}, u32[]{:S(2)}) copy-start(f32[128]{0:T(128)S(1)} %rsqrt.12) | copy-start | bytes 1540
  108.5 193.3 %all-reduce.5.cloned.1.call-start = ((), (), s32[]{:S(2)}) async-start(), calls=%async_computation.4 | async-start | bytes 229376 | tf_op jit(solution)/shard_map/psum | solution.py:130
  114.1 68.8 %collective-permute-start.2 = (f32[3,32,512]{2,1,0:T(8,128)S(1)}, f32[3,32,512]{2,1,0:T(8,128)S(1)}, u32[]{:S(2)}, u32[]{:S(2)}) collective-permute-start(f32[3,32,512]{2,1,0:T(8,128)S(1)} %bitcast.203), channel_id=1, source_target_pairs={{0,1},{1,2},{2,3},{3,4},{4,5},{5,6},{6,7},{7,8},{8,9},{9,10},{10,1... | collective-permute-start | bytes 589832 | tf_op jit(solution)/shard_map/ppermute | solution.py:14
  116.3 66.5 %collective-permute-start.3 = (f32[3,32,512]{2,1,0:T(8,128)S(1)}, f32[3,32,512]{2,1,0:T(8,128)S(1)}, u32[]{:S(2)}, u32[]{:S(2)}) collective-permute-start(f32[3,32,512]{2,1,0:T(8,128)S(1)} %bitcast.202), channel_id=1, source_target_pairs={{1,0},{2,1},{3,2},{4,3},{5,4},{6,5},{7,6},{8,7},{9,8},{10,9},{11,1... | collective-permute-start | bytes 589832 | tf_op jit(solution)/shard_map/ppermute | solution.py:17
  118.1 64.8 %copy-start.12 = (f32[1,1,512]{2,1,0:T(1,128)S(1)}, f32[1,1,512]{2,1,0:T(1,128)}, u32[]{:S(2)}) copy-start(f32[1,1,512]{2,1,0:T(1,128)} %copy-done.11) | copy-start | bytes 6148
  118.1 64.8 %copy-start.14 = (f32[1,1,512]{2,1,0:T(1,128)S(1)}, f32[1,1,512]{2,1,0:T(1,128)}, u32[]{:S(2)}) copy-start(f32[1,1,512]{2,1,0:T(1,128)} %copy-done.13) | copy-start | bytes 6148
  118.2 64.8 %copy-start.16 = (f32[1,1,512]{2,1,0:T(1,128)S(1)}, f32[1,1,512]{2,1,0:T(1,128)}, u32[]{:S(2)}) copy-start(f32[1,1,512]{2,1,0:T(1,128)} %copy-done.15) | copy-start | bytes 6148
  118.2 64.8 %copy-start.18 = (f32[1,1,512]{2,1,0:T(1,128)S(1)}, f32[1,1,512]{2,1,0:T(1,128)}, u32[]{:S(2)}) copy-start(f32[1,1,512]{2,1,0:T(1,128)} %copy-done.17) | copy-start | bytes 6148
  118.2 64.8 %copy-start.20 = (f32[1,1,512]{2,1,0:T(1,128)S(1)}, f32[1,1,512]{2,1,0:T(1,128)}, u32[]{:S(2)}) copy-start(f32[1,1,512]{2,1,0:T(1,128)} %copy-done.19) | copy-start | bytes 6148
  118.2 64.8 %copy-start.22 = (f32[1,1,512]{2,1,0:T(1,128)S(1)}, f32[1,1,512]{2,1,0:T(1,128)}, u32[]{:S(2)}) copy-start(f32[1,1,512]{2,1,0:T(1,128)} %copy-done.21) | copy-start | bytes 6148
  118.2 64.8 %copy-start.24 = (f32[1,1,512]{2,1,0:T(1,128)S(1)}, f32[1,1,512]{2,1,0:T(1,128)}, u32[]{:S(2)}) copy-start(f32[1,1,512]{2,1,0:T(1,128)} %copy-done.23) | copy-start | bytes 6148
  118.2 64.8 %copy-start.26 = (f32[1,1,512]{2,1,0:T(1,128)S(1)}, f32[1,1,512]{2,1,0:T(1,128)}, u32[]{:S(2)}) copy-start(f32[1,1,512]{2,1,0:T(1,128)} %copy-done.25) | copy-start | bytes 6148
  118.2 64.8 %copy-start.28 = (f32[1,1,512]{2,1,0:T(1,128)S(1)}, f32[1,1,512]{2,1,0:T(1,128)}, u32[]{:S(2)}) copy-start(f32[1,1,512]{2,1,0:T(1,128)} %copy-done.27) | copy-start | bytes 6148
  118.2 64.8 %copy-start.30 = (f32[1,1,512]{2,1,0:T(1,128)S(1)}, f32[1,1,512]{2,1,0:T(1,128)}, u32[]{:S(2)}) copy-start(f32[1,1,512]{2,1,0:T(1,128)} %copy-done.29) | copy-start | bytes 6148
  118.2 64.8 %copy-start.32 = (f32[1,1,512]{2,1,0:T(1,128)S(1)}, f32[1,1,512]{2,1,0:T(1,128)}, u32[]{:S(2)}) copy-start(f32[1,1,512]{2,1,0:T(1,128)} %copy-done.31) | copy-start | bytes 6148
  118.2 64.8 %copy-start.34 = (f32[1,1,512]{2,1,0:T(1,128)S(1)}, f32[1,1,512]{2,1,0:T(1,128)}, u32[]{:S(2)}) copy-start(f32[1,1,512]{2,1,0:T(1,128)} %copy-done.33) | copy-start | bytes 6148
  118.3 64.8 %copy-start.36 = (f32[1,1,512]{2,1,0:T(1,128)S(1)}, f32[1,1,512]{2,1,0:T(1,128)}, u32[]{:S(2)}) copy-start(f32[1,1,512]{2,1,0:T(1,128)} %copy-done.35) | copy-start | bytes 6148
  (47 other events, 858.9 us)
Sparse Core Ops, SparseCore 0:
  10.8 44.2 all-gather.2
  57.8 40.1 all-gather.4
  108.6 103.7 reduce-scatter.1
  216.3 85.4 all-reduce.4
where the time goes:
time: 312 us; the launch traced here: 310 us
  waiting for transfers between devices  186 us (60%)
  blocking collectives  62.8 us (20%)
  other arithmetic  16.1 us (5%)
  between operations  14.9 us (5%)
  matrix products  11.5 us (4%)
  local copies, waits for them, and re-layouts  10.9 us (3%)
  starting transfers between devices  7.42 us (2%)
    psum x1, waiting for transfers between devices, per_device(): lax.psum((kernel_term, norm_scale * gain_term, norm_scale * bias_term, no...  87.5 us
    psum x1, blocking collectives, per_device(): lax.psum((kernel_term, norm_scale * gain_term, norm_scale * bias_term, no...  62.8 us
    all_gather x1, waiting for transfers between devices, per_device(): lax.all_gather(out_narrow, 'row', axis=0, tiled=True)  40.8 us
    all_gather x1, waiting for transfers between devices, per_device(): lax.all_gather(in_narrow, 'row', axis=0, tiled=True)  31.1 us
    reduce_scatter x1, waiting for transfers between devices, per_device(): lax.psum_scatter(jnp.concatenate([norm_scale * contract_first(normed_out,...  26.6 us
    dot_general x2, matrix products, contract_last(): lax.dot_general(left, right, (((1,), (1,)), ((), ())), preferred_element_...  6.52 us
  transfers between devices with their start and end apart: 8, of which 4 were waited for; matrix products, arithmetic and copies ran while one was open for 7% of the time, Pallas kernels for 0%

commit v1 on v0

--- a/solution.py
+++ b/solution.py
@@ -1,8 +1,11 @@
+import functools
 import math
 
 import jax
 import jax.numpy as jnp
 from jax import lax
+from jax.experimental import pallas as pl
+from jax.experimental.pallas import tpu as pltpu
 from jax.sharding import PartitionSpec as P
 
 
@@ -150,9 +153,552 @@
     )
 
 
+F32, BF16 = jnp.float32, jnp.bfloat16
+MESH = pl.DeviceIdType.MESH
+CORES, XS = 2, 2
+LANES = 128
+EDGE = 8
+
+
+def fits(count):
+    planes = count // (CORES * XS)
+    return count % (CORES * XS) == 0 and planes == 4
+
+
+def per_device_fused(
+    features, cotangent, kernel, norm_gain, norm_bias, in_weight, in_bias, out_weight, layer_scale
+):
+    count = lax.axis_size("row")
+    planes = count // (CORES * XS)
+    rows, cols, channels = features.shape
+    own, hidden = in_weight.shape
+    pixels = rows * cols
+    taps = kernel.shape[0]
+    rim = taps // 2
+    wide = cols + 2 * EDGE
+    chunk = channels
+    pieces = hidden // chunk
+    tap_total = taps * taps
+    bias_rows = hidden // channels
+    small_rows = tap_total + 3 + bias_rows
+    norm_scale = 1.0 / math.sqrt(pixels * count)
+
+    def body(
+        feat, cot, kern, gain, beta, w_in, b_in, w_out, scale,
+        out, in_grad, gw_in, gw_out, small_out,
+        weights, grads, from_core, x_send, from_x, z_send, from_up, from_down, line_sum,
+        padded, grad_padded, grad_edge, conv, normed_s, inv_s, no_s, no_t, bg_s, bg_t, mixed_s, og_s,
+        small, from_small,
+        s_ag, r_ag, s_core, r_core, s_x, r_x, s_z, r_up, r_down,
+        s_halo, r_halo, s_ghalo, r_ghalo, s_small, r_small,
+    ):
+        me = lax.axis_index("row")
+        core = lax.rem(me, CORES)
+        xpos = lax.rem(me // CORES, XS)
+        z = me // (CORES * XS)
+        sibling = me + 1 - 2 * core
+        across = me + CORES - 2 * CORES * xpos
+        step_z = CORES * XS
+
+        def at(zz, xx, cc):
+            return (zz * XS + xx) * CORES + cc
+
+        def copy(src, dst, send, recv, target):
+            return pltpu.make_async_remote_copy(
+                src_ref=src, dst_ref=dst, send_sem=send, recv_sem=recv,
+                device_id={"row": target}, device_id_type=MESH,
+            )
+
+        has_up, has_down = z < planes - 1, z > 0
+        has_next, has_prev = me < count - 1, me > 0
+        far_z = z + 2 - 4 * lax.rem(z // 2, 2)
+        near_z = z + 1 - 2 * lax.rem(z, 2)
+        far, near = at(far_z, xpos, core), at(near_z, xpos, core)
+
+        weights[0, me] = w_in[...].astype(BF16)
+        weights[1, me] = w_out[...].astype(BF16)
+
+        barrier = pltpu.get_barrier_semaphore()
+
+        def greet(target):
+            pl.semaphore_signal(barrier, inc=1, device_id={"row": target}, device_id_type=MESH)
+
+        outer = lax.rem(me + count + 2 * core - 1, count)
+        peers = [sibling, across, outer]
+        peers += [at(lax.rem(z + d, planes), xpos, core) for d in range(1, planes)]
+        for target in peers:
+            greet(target)
+        pl.semaphore_wait(barrier, len(peers))
+
+        halo_next = copy(
+            feat.at[rows - rim :], padded.at[0:rim, EDGE : EDGE + cols],
+            s_halo.at[0], r_halo.at[0], lax.rem(me + 1, count),
+        )
+        halo_prev = copy(
+            feat.at[0:rim], padded.at[rows + rim :, EDGE : EDGE + cols],
+            s_halo.at[1], r_halo.at[1], lax.rem(me + count - 1, count),
+        )
+
+        @pl.when(has_next)
+        def _():
+            halo_next.start()
+
+        @pl.when(has_prev)
+        def _():
+            halo_prev.start()
+
+        def block(r):
+            return weights.at[:, r]
+
+        def ag(r, way, target):
+            return copy(block(r), block(r), s_ag.at[way, r], r_ag.at[r], target)
+
+        def arrived(r):
+            ag(r, 0, sibling).wait_recv()
+
+        started = []
+
+        def send_if(here, r, way, target):
+            if here is True:
+                ag(r, way, target).start()
+            else:
+                @pl.when(here)
+                def _():
+                    ag(r, way, target).start()
+            started.append((here, r, way, target))
+
+        send_if(has_up, me, 0, me + step_z)
+        send_if(has_down, me, 1, me - step_z)
+        send_if(True, me, 2, across)
+        send_if(True, me, 3, sibling)
+
+        def gather_line(d):
+            for sign in (1, -1):
+                zz = z - sign * d
+                here = (zz >= 0) & (zz < planes)
+                r = at(zz, xpos, core)
+                onward = has_up if sign > 0 else has_down
+
+                @pl.when(here)
+                def _():
+                    arrived(r)
+
+                send_if(here & onward, r, 0 if sign > 0 else 1, me + sign * step_z)
+                send_if(here, r, 2, across)
+                send_if(here, r, 3, sibling)
+
+        def gather_across(d):
+            for sign in (1, -1) if d else (1,):
+                zz = z - sign * d
+                here = (zz >= 0) & (zz < planes)
+                r = at(zz, 1 - xpos, core)
+
+                @pl.when(here)
+                def _():
+                    arrived(r)
+
+                send_if(here, r, 3, sibling)
+
+        blank = jnp.zeros((rows + 2 * rim, EDGE, channels), F32)
+        for pad in (padded, grad_padded):
+            pad[:, 0:EDGE, :] = blank
+            pad[:, EDGE + cols :, :] = blank
+        no_rows = jnp.zeros((rim, cols, channels), F32)
+        padded[rim : rim + rows, EDGE : EDGE + cols, :] = feat[...]
+        for here, first in ((has_prev, 0), (has_next, rows + rim)):
+            @pl.when(jnp.logical_not(here))
+            def _():
+                padded[first : first + rim, EDGE : EDGE + cols, :] = no_rows
+                grad_padded[first : first + rim, EDGE : EDGE + cols, :] = no_rows
+        scaled = scale[...] * cot[...].reshape(pixels, channels)
+        bg_s[...] = scaled.astype(BF16)
+        bg_t[...] = scaled.T.astype(BF16)
+
+        @pl.when(has_prev)
+        def _():
+            halo_next.wait_recv()
+
+        @pl.when(has_next)
+        def _():
+            halo_prev.wait_recv()
+
+        def lanes_of(i):
+            return pl.ds(pl.multiple_of(i * LANES, LANES), LANES)
+
+        def tap_sums(source, lanes, flip, starts):
+            sums = list(starts)
+            for j in range(taps):
+                shift = EDGE - rim + j
+                lines = [source[q, shift : shift + cols, lanes] for q in range(rows + 2 * rim)]
+                for i in range(taps):
+                    t = (taps - 1 - i) * taps + taps - 1 - j if flip else i * taps + j
+                    weight = kern[t : t + 1, lanes]
+                    for q in range(rows):
+                        sums[q] = sums[q] + lines[q + i] * weight
+            return sums
+
+        def conv_step(i, carry):
+            lanes = lanes_of(i)
+            sums = tap_sums(padded, lanes, False, [jnp.zeros((cols, LANES), F32)] * rows)
+            for q in range(rows):
+                conv[q * cols : (q + 1) * cols, lanes] = sums[q]
+            return carry
+
+        lax.fori_loop(0, channels // LANES, conv_step, 0)
+        gather_line(1)
+        value = conv[...]
+        centred = value - jnp.mean(value, axis=1, keepdims=True)
+        inv_std = lax.rsqrt(jnp.mean(centred * centred, axis=1, keepdims=True) + 1e-06)
+        normed = centred * inv_std
+        normed_s[...] = normed
+        inv_s[...] = jnp.broadcast_to(inv_std, inv_s.shape)
+        rescaled = normed * gain[...] + beta[...]
+        no_s[...] = rescaled.astype(BF16)
+        no_t[...] = rescaled.T.astype(BF16)
+        mixed_s[...] = jnp.zeros_like(mixed_s)
+        og_s[...] = jnp.zeros_like(og_s)
+        gather_across(0)
+        for d in range(2, planes):
+            gather_line(d)
+            gather_across(d - 1)
+        gather_across(planes - 1)
+        for xx in (xpos, 1 - xpos):
+            for zz in range(planes):
+                arrived(at(zz, xx, 1 - core))
+
+        def last_last(a, b):
+            return lax.dot_general(a, b, (((1,), (1,)), ((), ())), preferred_element_type=F32)
+
+        def mlp_step(p, carry):
+            span = pl.ds(pl.multiple_of(p * chunk, chunk), chunk)
+            win = weights[0, :, :, span].reshape(channels, chunk)
+            wout = weights[1, :, :, span].reshape(channels, chunk)
+            preact = jnp.dot(no_s[...], win, preferred_element_type=F32) + b_in[:, span]
+            cdf = 0.5 * (1.0 + lax.erf(preact * 0.7071067811865476))
+            activated = (preact * cdf).astype(BF16)
+            act_grad = jnp.dot(bg_s[...], wout, preferred_element_type=F32)
+            slope = cdf + preact * jnp.exp(-0.5 * preact * preact) * 0.3989422804014327
+            hidden_grad = act_grad * slope
+            small[pl.ds(tap_total + 3 + p, 1), :] = norm_scale * jnp.sum(
+                hidden_grad, axis=0, keepdims=True
+            )
+            narrow = hidden_grad.astype(BF16)
+            grads[:, 0, :, span] = (
+                (norm_scale * jnp.dot(no_t[...], narrow, preferred_element_type=F32))
+                .astype(BF16).reshape(count, own, chunk)
+            )
+            grads[:, 1, :, span] = (
+                (norm_scale * jnp.dot(bg_t[...], activated, preferred_element_type=F32))
+                .astype(BF16).reshape(count, own, chunk)
+            )
+            mixed_s[...] += last_last(activated, wout)
+            og_s[...] += last_last(narrow, win)
+            return carry
+
+        lax.fori_loop(0, pieces, mlp_step, 0)
+
+        order = []
+        for d in range(planes - 1, 0, -1):
+            for sign in (1, -1):
+                zz = z + sign * d
+                order.append((zz, (zz >= 0) & (zz < planes), sign))
+
+        def each(run, xx):
+            for zz, here, sign in order:
+                @pl.when(here)
+                def _():
+                    run(zz, xx, sign)
+            run(z, xx, 0)
+
+        def core_copy(zz, xx):
+            slot = zz * XS + xx
+            return copy(
+                grads.at[at(zz, xx, 1 - core)], from_core.at[slot],
+                s_core.at[slot], r_core.at[slot], sibling,
+            )
+
+        def x_copy(zz):
+            return copy(x_send.at[zz], from_x.at[zz], s_x.at[zz], r_x.at[zz], across)
+
+        def up_copy(zz):
+            return copy(
+                z_send.at[zz], from_up.at[zz], s_z.at[zz], r_up.at[zz],
+                at(lax.rem(z + 1, planes), xpos, core),
+            )
+
+        def down_copy(zz):
+            return copy(
+                z_send.at[zz], from_down.at[zz], s_z.at[zz], r_down.at[zz],
+                at(lax.rem(z + planes - 1, planes), xpos, core),
+            )
+
+        each(lambda zz, xx, sign: core_copy(zz, xx).start(), 1 - xpos)
+        each(lambda zz, xx, sign: core_copy(zz, xx).start(), xpos)
+
+        flat_cot = cot[...].reshape(pixels, channels)
+        mixed = mixed_s[...]
+        out[...] = feat[...] + (scale[...] * mixed).reshape(rows, cols, channels)
+        small[tap_total + 2 : tap_total + 3, :] = norm_scale * jnp.sum(
+            flat_cot * mixed, axis=0, keepdims=True
+        )
+        out_grad = og_s[...]
+        normed = normed_s[...]
+        small[tap_total : tap_total + 1, :] = norm_scale * jnp.sum(
+            out_grad * normed, axis=0, keepdims=True
+        )
+        small[tap_total + 1 : tap_total + 2, :] = norm_scale * jnp.sum(
+            out_grad, axis=0, keepdims=True
+        )
+        normed_grad = out_grad * gain[...]
+        conv_grad = inv_s[:, 0:1] * (
+            normed_grad
+            - jnp.mean(normed_grad, axis=1, keepdims=True)
+            - normed * jnp.mean(normed_grad * normed, axis=1, keepdims=True)
+        )
+        grid = conv_grad.reshape(rows, cols, channels)
+        grad_padded[rim : rim + rows, EDGE : EDGE + cols, :] = grid
+        grad_edge[...] = grid
+        ghalo_next = copy(
+            grad_edge.at[rows - rim :], grad_padded.at[0:rim, EDGE : EDGE + cols],
+            s_ghalo.at[0], r_ghalo.at[0], lax.rem(me + 1, count),
+        )
+        ghalo_prev = copy(
+            grad_edge.at[0:rim], grad_padded.at[rows + rim :, EDGE : EDGE + cols],
+            s_ghalo.at[1], r_ghalo.at[1], lax.rem(me + count - 1, count),
+        )
+
+        @pl.when(has_next)
+        def _():
+            ghalo_next.start()
+
+        @pl.when(has_prev)
+        def _():
+            ghalo_prev.start()
+
+        def add_for_x(zz, xx, sign):
+            core_copy(zz, xx).wait_recv()
+            x_send[zz] = (
+                grads[at(zz, xx, core)].astype(F32) + from_core[zz * XS + xx].astype(F32)
+            ).astype(BF16)
+            x_copy(zz).start()
+
+        each(add_for_x, 1 - xpos)
+
+        def kernel_step(i, carry):
+            lanes = lanes_of(i)
+            lines_grad = [grad_edge[q, :, lanes] for q in range(rows)]
+            for j in range(taps):
+                shift = EDGE - rim + j
+                lines = [padded[q, shift : shift + cols, lanes] for q in range(rows + 2 * rim)]
+                for k in range(taps):
+                    total = lines[k] * lines_grad[0]
+                    for q in range(1, rows):
+                        total = total + lines[k + q] * lines_grad[q]
+                    t = k * taps + j
+                    small[t : t + 1, lanes] = norm_scale * jnp.sum(total, axis=0, keepdims=True)
+            return carry
+
+        lax.fori_loop(0, channels // LANES, kernel_step, 0)
+
+        hops = (sibling, across, near, far)
+
+        def small_copy(h):
+            return copy(
+                small.at[h * small_pad : (h + 1) * small_pad], from_small.at[h],
+                s_small.at[h], r_small.at[h], hops[h],
+            )
+
+        def small_add(h):
+            small_copy(h).wait_recv()
+            small[(h + 1) * small_pad : (h + 2) * small_pad] = (
+                small[h * small_pad : (h + 1) * small_pad] + from_small[h]
+            )
+            if h + 1 < len(hops):
+                small_copy(h + 1).start()
+
+        small_copy(0).start()
+
+        def add_for_line(zz, xx, sign):
+            core_copy(zz, xx).wait_recv()
+            line_sum[zz] = grads[at(zz, xx, core)].astype(F32) + from_core[zz * XS + xx].astype(F32)
+
+        each(add_for_line, xpos)
+        small_add(0)
+
+        @pl.when(has_prev)
+        def _():
+            ghalo_next.wait_recv()
+
+        @pl.when(has_next)
+        def _():
+            ghalo_prev.wait_recv()
+
+        def back_step(i, carry):
+            lanes = lanes_of(i)
+            sums = tap_sums(grad_padded, lanes, True, [cot[q, :, lanes] for q in range(rows)])
+            for q in range(rows):
+                in_grad[q, :, lanes] = sums[q]
+            return carry
+
+        lax.fori_loop(0, channels // LANES, back_step, 0)
+        small_add(1)
+
+        def pass_on(zz, sign):
+            x_copy(zz).wait_recv()
+            line_sum[zz] = line_sum[zz] + from_x[zz].astype(F32)
+            if sign > 0:
+                @pl.when(has_down)
+                def _():
+                    up_copy(zz).wait_recv()
+                    line_sum[zz] = line_sum[zz] + from_up[zz].astype(F32)
+                z_send[zz] = line_sum[zz].astype(BF16)
+                up_copy(zz).start()
+            else:
+                @pl.when(has_up)
+                def _():
+                    down_copy(zz).wait_recv()
+                    line_sum[zz] = line_sum[zz] + from_down[zz].astype(F32)
+                z_send[zz] = line_sum[zz].astype(BF16)
+                down_copy(zz).start()
+
+        for number, (zz, here, sign) in enumerate(order):
+            @pl.when(here)
+            def _():
+                pass_on(zz, sign)
+            if number == 1:
+                small_add(2)
+        small_add(3)
+        small_out[...] = small[4 * small_pad : 5 * small_pad]
+        x_copy(z).wait_recv()
+        line_sum[z] = line_sum[z] + from_x[z].astype(F32)
+
+        @pl.when(has_down)
+        def _():
+            up_copy(z).wait_recv()
+            line_sum[z] = line_sum[z] + from_up[z].astype(F32)
+
+        @pl.when(has_up)
+        def _():
+            down_copy(z).wait_recv()
+            line_sum[z] = line_sum[z] + from_down[z].astype(F32)
+
+        gw_in[...] = line_sum[z, 0]
+        gw_out[...] = line_sum[z, 1]
+
+        @pl.when(has_next)
+        def _():
+            halo_next.wait_send()
+            ghalo_next.wait_send()
+
+        @pl.when(has_prev)
+        def _():
+            halo_prev.wait_send()
+            ghalo_prev.wait_send()
+
+        for here, r, way, target in started:
+            if here is True:
+                ag(r, way, target).wait_send()
+            else:
+                @pl.when(here)
+                def _():
+                    ag(r, way, target).wait_send()
+        for zz in range(planes):
+            for xx in range(XS):
+                core_copy(zz, xx).wait_send()
+            x_copy(zz).wait_send()
+        for zz, here, sign in order:
+            @pl.when(here)
+            def _():
+                up_copy(zz).wait_send()
+        for h in range(len(hops)):
+            small_copy(h).wait_send()
+
+    small_pad = -(-small_rows // 8) * 8
+    vmem = pl.BlockSpec(memory_space=pltpu.VMEM)
+    dma = pltpu.SemaphoreType.DMA
+    whole = (rows + 2 * rim, wide, channels)
+    pair = (2, own, hidden)
+    results = pl.pallas_call(
+        body,
+        out_shape=(
+            jax.ShapeDtypeStruct(features.shape, F32),
+            jax.ShapeDtypeStruct(features.shape, F32),
+            jax.ShapeDtypeStruct((own, hidden), F32),
+            jax.ShapeDtypeStruct((own, hidden), F32),
+            jax.ShapeDtypeStruct((small_pad, channels), F32),
+        ),
+        in_specs=[vmem] * 9,
+        out_specs=[vmem] * 5,
+        scratch_shapes=[
+            pltpu.VMEM((2, count, own, hidden), BF16),
+            pltpu.VMEM((count,) + pair, BF16),
+            pltpu.VMEM((planes * XS,) + pair, BF16),
+            pltpu.VMEM((planes,) + pair, BF16),
+            pltpu.VMEM((planes,) + pair, BF16),
+            pltpu.VMEM((planes,) + pair, BF16),
+            pltpu.VMEM((planes,) + pair, BF16),
+            pltpu.VMEM((planes,) + pair, BF16),
+            pltpu.VMEM((planes,) + pair, F32),
+            pltpu.VMEM(whole, F32),
+            pltpu.VMEM(whole, F32),
+            pltpu.VMEM(features.shape, F32),
+            pltpu.VMEM((pixels, channels), F32),
+            pltpu.VMEM((pixels, channels), F32),
+            pltpu.VMEM((pixels, LANES), F32),
+            pltpu.VMEM((pixels, channels), BF16),
+            pltpu.VMEM((channels, pixels), BF16),
+            pltpu.VMEM((pixels, channels), BF16),
+            pltpu.VMEM((channels, pixels), BF16),
+            pltpu.VMEM((pixels, channels), F32),
+            pltpu.VMEM((pixels, channels), F32),
+            pltpu.VMEM((5 * small_pad, channels), F32),
+            pltpu.VMEM((4, small_pad, channels), F32),
+            dma((4, count)),
+            dma((count,)),
+            dma((planes * XS,)),
+            dma((planes * XS,)),
+            dma((planes,)),
+            dma((planes,)),
+            dma((planes,)),
+            dma((planes,)),
+            dma((planes,)),
+            dma((2,)),
+            dma((2,)),
+            dma((2,)),
+            dma((2,)),
+            dma((4,)),
+            dma((4,)),
+        ],
+        compiler_params=pltpu.CompilerParams(collective_id=0, has_side_effects=True),
+        name="convnext_block",
+    )(
+        features,
+        cotangent,
+        kernel.reshape(tap_total, channels),
+        norm_gain.reshape(1, channels),
+        norm_bias.reshape(1, channels),
+        in_weight,
+        in_bias.reshape(1, hidden),
+        out_weight,
+        layer_scale.reshape(1, channels),
+    )
+    output, input_grad, in_weight_grad, out_weight_grad, sums = results
+    return (
+        output,
+        input_grad,
+        in_weight_grad,
+        out_weight_grad,
+        sums[:tap_total].reshape(taps, taps, channels),
+        sums[tap_total],
+        sums[tap_total + 1],
+        sums[tap_total + 3 : small_rows].reshape(hidden),
+        sums[tap_total + 2],
+    )
+
+
 def solution(mesh):
     return jax.shard_map(
-        per_device,
+        per_device_fused if fits(mesh.shape["row"]) else per_device,
         mesh=mesh,
         in_specs=(
             P(("grp", "row"), None, None),

time: 312 us -> 111 us (0.36)
  waiting for transfers between devices: 186 us -> 0 us
  Pallas kernels: 0 us -> 100 us
  blocking collectives: 62.8 us -> 0 us
  other arithmetic: 16.1 us -> 0 us
  between operations: 14.9 us -> 0.67 us
  matrix products: 11.5 us -> 0 us
  starting transfers between devices: 7.42 us -> 0 us
    pallas_call x0 -> x1, Pallas kernels: none -> 100 us  [per_device_fused(): pl.pallas_call(body, out_shape=(jax.ShapeDtypeStruct(features.shape, F32)...]
    psum x1 -> x0, waiting for transfers between devices: 87.5 us -> none  [per_device(): lax.psum((kernel_term, norm_scale * gain_term, norm_scale * bias_term, no...]
    all_gather x2 -> x0, waiting for transfers between devices: 71.9 us -> none  [the longest x1 40.8 us: per_device(): lax.all_gather(out_narrow, 'row', axis=0, tiled=True)]
    psum x1 -> x0, blocking collectives: 62.8 us -> none  [per_device(): lax.psum((kernel_term, norm_scale * gain_term, norm_scale * bias_term, no...]
    reduce_scatter x1 -> x0, waiting for transfers between devices: 26.6 us -> none  [per_device(): lax.psum_scatter(jnp.concatenate([norm_scale * contract_first(normed_out,...]
    dot_general x6 -> x0, matrix products: 11.5 us -> none  [the longest x2 6.52 us: contract_last(): lax.dot_general(left, right, (((1,), (1,)), ((), ())), preferred_element_...]
    ppermute x4 -> x0, starting transfers between devices: 7.26 us -> none  [the longest x2 4.54 us: extended(): lax.ppermute(lax.slice_in_dim(block, block.shape[dim] - width, None, axis...]
    concatenate x3 -> x0, other arithmetic: 5.17 us -> none  [the longest x1 3.76 us: per_device(): jnp.concatenate([norm_scale * contract_first(normed_out, hidden_narrow),...]
  transfers between devices with their start and end apart: 8 -> 0, of which waited for: 4 -> 0; matrix products, arithmetic and copies ran while one was open for 7% -> 0% of each run, Pallas kernels for 0% -> 0%
where the time goes in v1:
time: 111 us
  Pallas kernels  100 us (90%)
  local copies, waits for them, and re-layouts  9.74 us (9%)
    pallas_call x1, Pallas kernels, per_device_fused(): pl.pallas_call(body, out_shape=(jax.ShapeDtypeStruct(features.shape, F32)...  100 us
    unnamed x14, local copies, waits for them, and re-layouts  5.16 us

profile of v1, /device:TPU:0, one launch (start us, length us, event | category | flops | bytes accessed | tf_op | source)
XLA Modules:
  0.0 110.7 jit_solution(10440826781323570584)
XLA Ops:
  0.6 1.6 %reshape.39.kern = f32[49,512]{1,0:T(8,128)} reshape(f32[7,7,512]{2,1,0:T(8,128)} %param.11) | data formatting | bytes 200704 | tf_op jit(solution)/shard_map/reshape | solution.py:677
  2.2 100.3 %convnext_block.1 = (f32[4,32,512]{2,1,0:T(8,128)}, f32[4,32,512]{2,1,0:T(8,128)}, f32[32,2048]{1,0:T(8,128)}, f32[32,2048]{1,0:T(8,128)}, f32[56,512]{1,0:T(8,128)}) custom-call(f32[4,32,512]{2,1,0:T(8,128)} %feat.1, f32[4,32,512]{2,1,0:T(8,128)} %cot.1, f32[49,512]{1,0:T(8,128)} %reshape.39.kern, f32[1,512]{1,0:T(1,128)} %bitcast.14, f32[1,512]{1,0:T(1,128)} %bitcast.15, ...), custom_call_target="tpu_custom_call" | custom-call | tf_op jit(solution)/shard_map/convnext_block/pallas_call | solution.py:621
  102.5 0.0 copy-start.3
  102.5 1.6 %reshape.44 = f32[7,7,512]{2,1,0:T(8,128)} reshape(f32[49,512]{1,0:T(8,128)} %bitcast.11) | data formatting | bytes 200704 | tf_op jit(solution)/shard_map/reshape | solution.py:691
  104.1 1.4 %fusion = (f32[1,512]{1,0:T(1,128)}, f32[1,512]{1,0:T(1,128)}, f32[1,512]{1,0:T(1,128)}) fusion(f32[56,512]{1,0:T(8,128)} %get-tuple-element.18), kind=kLoop, calls=%fused_computation.1 | loop fusion | bytes 12288 | tf_op jit(solution)/shard_map/slice | solution.py:695
  105.5 0.7 slice_bitcast_fusion
  106.2 0.6 copy.18
  106.8 0.0 copy-done.3
  106.8 0.0 copy-start.2
  106.8 0.7 copy.23
  107.5 0.3 copy-done.2
  107.9 0.0 copy-start.1
  107.9 0.7 copy.24
  108.6 0.3 copy-done.1
  108.9 0.0 copy-start
  108.9 0.7 copy.25
  109.6 0.3 copy-done
  110.0 0.7 copy.26
Async XLA Ops:
  102.5 4.4 %copy-start.3 = (f32[4,32,512]{2,1,0:T(8,128)S(1)}, f32[4,32,512]{2,1,0:T(8,128)}, u32[]{:S(2)}) copy-start(f32[4,32,512]{2,1,0:T(8,128)} %get-tuple-element.31) | copy-start | bytes 786436
  106.8 1.0 copy-start.2
  107.9 1.0 copy-start.1
  108.9 1.0 copy-start

commit v2 on v1

--- a/solution.py
+++ b/solution.py
@@ -185,9 +185,9 @@
 
     def body(
         feat, cot, kern, gain, beta, w_in, b_in, w_out, scale,
-        out, in_grad, gw_in, gw_out, small_out,
-        weights, grads, from_core, x_send, from_x, z_send, from_up, from_down, line_sum,
-        padded, grad_padded, grad_edge, conv, normed_s, inv_s, no_s, no_t, bg_s, bg_t, mixed_s, og_s,
+        out, in_grad, gw_in, gw_out, taps_out, small_out,
+        weights, grads, from_core, x_send, from_x, z_send, from_up, from_down,
+        padded, grad_padded, grad_edge, feat_edge, edge_in, conv, normed_s, inv_s, no_s, no_t, bg_s, bg_t, mixed_s, og_s,
         small, from_small,
         s_ag, r_ag, s_core, r_core, s_x, r_x, s_z, r_up, r_down,
         s_halo, r_halo, s_ghalo, r_ghalo, s_small, r_small,
@@ -215,6 +215,7 @@
         near_z = z + 1 - 2 * lax.rem(z, 2)
         far, near = at(far_z, xpos, core), at(near_z, xpos, core)
 
+        feat_edge[...] = feat[...].astype(BF16)
         weights[0, me] = w_in[...].astype(BF16)
         weights[1, me] = w_out[...].astype(BF16)
 
@@ -231,11 +232,11 @@
         pl.semaphore_wait(barrier, len(peers))
 
         halo_next = copy(
-            feat.at[rows - rim :], padded.at[0:rim, EDGE : EDGE + cols],
+            feat_edge.at[rows - rim :], edge_in.at[0],
             s_halo.at[0], r_halo.at[0], lax.rem(me + 1, count),
         )
         halo_prev = copy(
-            feat.at[0:rim], padded.at[rows + rim :, EDGE : EDGE + cols],
+            feat_edge.at[0:rim], edge_in.at[1],
             s_halo.at[1], r_halo.at[1], lax.rem(me + count - 1, count),
         )
 
@@ -317,10 +318,12 @@
         @pl.when(has_prev)
         def _():
             halo_next.wait_recv()
+            padded[0:rim, EDGE : EDGE + cols, :] = edge_in[0].astype(F32)
 
         @pl.when(has_next)
         def _():
             halo_prev.wait_recv()
+            padded[rows + rim :, EDGE : EDGE + cols, :] = edge_in[1].astype(F32)
 
         def lanes_of(i):
             return pl.ds(pl.multiple_of(i * LANES, LANES), LANES)
@@ -331,8 +334,8 @@
                 shift = EDGE - rim + j
                 lines = [source[q, shift : shift + cols, lanes] for q in range(rows + 2 * rim)]
                 for i in range(taps):
-                    t = (taps - 1 - i) * taps + taps - 1 - j if flip else i * taps + j
-                    weight = kern[t : t + 1, lanes]
+                    ki, kj = (taps - 1 - i, taps - 1 - j) if flip else (i, j)
+                    weight = kern[ki, kj : kj + 1, lanes]
                     for q in range(rows):
                         sums[q] = sums[q] + lines[q + i] * weight
             return sums
@@ -432,14 +435,31 @@
                 at(lax.rem(z + planes - 1, planes), xpos, core),
             )
 
+        far_order = order[: 2 * (planes - 2)]
+        near_order = order[2 * (planes - 2) :]
+
+        def each_of(entries, run, xx):
+            for zz, here, sign in entries:
+                @pl.when(here)
+                def _():
+                    run(zz, xx, sign)
+
         each(lambda zz, xx, sign: core_copy(zz, xx).start(), 1 - xpos)
         each(lambda zz, xx, sign: core_copy(zz, xx).start(), xpos)
 
+        def pair_sum(zz, xx):
+            core_copy(zz, xx).wait_recv()
+            return grads[at(zz, xx, core)].astype(F32) + from_core[zz * XS + xx].astype(F32)
+
+        def add_for_x(zz, xx, sign):
+            x_send[zz] = pair_sum(zz, xx).astype(BF16)
+            x_copy(zz).start()
+
+        each_of(far_order, add_for_x, 1 - xpos)
+
         flat_cot = cot[...].reshape(pixels, channels)
-        mixed = mixed_s[...]
-        out[...] = feat[...] + (scale[...] * mixed).reshape(rows, cols, channels)
         small[tap_total + 2 : tap_total + 3, :] = norm_scale * jnp.sum(
-            flat_cot * mixed, axis=0, keepdims=True
+            flat_cot * mixed_s[...], axis=0, keepdims=True
         )
         out_grad = og_s[...]
         normed = normed_s[...]
@@ -457,13 +477,13 @@
         )
         grid = conv_grad.reshape(rows, cols, channels)
         grad_padded[rim : rim + rows, EDGE : EDGE + cols, :] = grid
-        grad_edge[...] = grid
+        grad_edge[...] = grid.astype(BF16)
         ghalo_next = copy(
-            grad_edge.at[rows - rim :], grad_padded.at[0:rim, EDGE : EDGE + cols],
+            grad_edge.at[rows - rim :], edge_in.at[2],
             s_ghalo.at[0], r_ghalo.at[0], lax.rem(me + 1, count),
         )
         ghalo_prev = copy(
-            grad_edge.at[0:rim], grad_padded.at[rows + rim :, EDGE : EDGE + cols],
+            grad_edge.at[0:rim], edge_in.at[3],
             s_ghalo.at[1], r_ghalo.at[1], lax.rem(me + count - 1, count),
         )
 
@@ -474,19 +494,12 @@
         @pl.when(has_prev)
         def _():
             ghalo_prev.start()
-
-        def add_for_x(zz, xx, sign):
-            core_copy(zz, xx).wait_recv()
-            x_send[zz] = (
-                grads[at(zz, xx, core)].astype(F32) + from_core[zz * XS + xx].astype(F32)
-            ).astype(BF16)
-            x_copy(zz).start()
-
-        each(add_for_x, 1 - xpos)
 
         def kernel_step(i, carry):
             lanes = lanes_of(i)
-            lines_grad = [grad_edge[q, :, lanes] for q in range(rows)]
+            lines_grad = [
+                grad_padded[rim + q, EDGE : EDGE + cols, lanes] for q in range(rows)
+            ]
             for j in range(taps):
                 shift = EDGE - rim + j
                 lines = [padded[q, shift : shift + cols, lanes] for q in range(rows + 2 * rim)]
@@ -517,21 +530,42 @@
                 small_copy(h + 1).start()
 
         small_copy(0).start()
-
-        def add_for_line(zz, xx, sign):
-            core_copy(zz, xx).wait_recv()
-            line_sum[zz] = grads[at(zz, xx, core)].astype(F32) + from_core[zz * XS + xx].astype(F32)
-
-        each(add_for_line, xpos)
+        out[...] = feat[...] + (scale[...] * mixed_s[...]).reshape(rows, cols, channels)
         small_add(0)
+        each_of(near_order, add_for_x, 1 - xpos)
+        add_for_x(z, 1 - xpos, 0)
+
+        def pass_on(zz, xx, sign):
+            fed, arriving, leaving = (
+                (has_down, up_copy(zz), up_copy(zz)) if sign > 0
+                else (has_up, down_copy(zz), down_copy(zz))
+            )
+            slots = from_up if sign > 0 else from_down
+            x_copy(zz).wait_recv()
+            total = pair_sum(zz, xx) + from_x[zz].astype(F32)
+
+            @pl.when(fed)
+            def _():
+                arriving.wait_recv()
+                z_send[zz] = (total + slots[zz].astype(F32)).astype(BF16)
+
+            @pl.when(jnp.logical_not(fed))
+            def _():
+                z_send[zz] = total.astype(BF16)
+
+            leaving.start()
+
+        each_of(far_order, pass_on, xpos)
 
         @pl.when(has_prev)
         def _():
             ghalo_next.wait_recv()
+            grad_padded[0:rim, EDGE : EDGE + cols, :] = edge_in[2].astype(F32)
 
         @pl.when(has_next)
         def _():
             ghalo_prev.wait_recv()
+            grad_padded[rows + rim :, EDGE : EDGE + cols, :] = edge_in[3].astype(F32)
 
         def back_step(i, carry):
             lanes = lanes_of(i)
@@ -542,48 +576,32 @@
 
         lax.fori_loop(0, channels // LANES, back_step, 0)
         small_add(1)
-
-        def pass_on(zz, sign):
-            x_copy(zz).wait_recv()
-            line_sum[zz] = line_sum[zz] + from_x[zz].astype(F32)
-            if sign > 0:
-                @pl.when(has_down)
-                def _():
-                    up_copy(zz).wait_recv()
-                    line_sum[zz] = line_sum[zz] + from_up[zz].astype(F32)
-                z_send[zz] = line_sum[zz].astype(BF16)
-                up_copy(zz).start()
-            else:
-                @pl.when(has_up)
-                def _():
-                    down_copy(zz).wait_recv()
-                    line_sum[zz] = line_sum[zz] + from_down[zz].astype(F32)
-                z_send[zz] = line_sum[zz].astype(BF16)
-                down_copy(zz).start()
-
-        for number, (zz, here, sign) in enumerate(order):
-            @pl.when(here)
-            def _():
-                pass_on(zz, sign)
-            if number == 1:
-                small_add(2)
+        each_of(near_order, pass_on, xpos)
+        small_add(2)
+        x_copy(z).wait_recv()
+        mine = pair_sum(z, xpos) + from_x[z].astype(F32)
+        gw_in[...] = mine[0]
+        gw_out[...] = mine[1]
+
+        def join(slots):
+            gw_in[...] += slots[z, 0].astype(F32)
+            gw_out[...] += slots[z, 1].astype(F32)
+
         small_add(3)
-        small_out[...] = small[4 * small_pad : 5 * small_pad]
-        x_copy(z).wait_recv()
-        line_sum[z] = line_sum[z] + from_x[z].astype(F32)
+        last = 4 * small_pad
+        for i in range(taps):
+            taps_out[i] = small[last + i * taps : last + (i + 1) * taps]
+        small_out[0 : small_rows - tap_total] = small[last + tap_total : last + small_rows]
 
         @pl.when(has_down)
         def _():
             up_copy(z).wait_recv()
-            line_sum[z] = line_sum[z] + from_up[z].astype(F32)
+            join(from_up)
 
         @pl.when(has_up)
         def _():
             down_copy(z).wait_recv()
-            line_sum[z] = line_sum[z] + from_down[z].astype(F32)
-
-        gw_in[...] = line_sum[z, 0]
-        gw_out[...] = line_sum[z, 1]
+            join(from_down)
 
         @pl.when(has_next)
         def _():
@@ -625,10 +643,11 @@
             jax.ShapeDtypeStruct(features.shape, F32),
             jax.ShapeDtypeStruct((own, hidden), F32),
             jax.ShapeDtypeStruct((own, hidden), F32),
-            jax.ShapeDtypeStruct((small_pad, channels), F32),
+            jax.ShapeDtypeStruct(kernel.shape, F32),
+            jax.ShapeDtypeStruct((small_rows - tap_total, channels), F32),
         ),
         in_specs=[vmem] * 9,
-        out_specs=[vmem] * 5,
+        out_specs=[vmem] * 6,
         scratch_shapes=[
             pltpu.VMEM((2, count, own, hidden), BF16),
             pltpu.VMEM((count,) + pair, BF16),
@@ -638,10 +657,11 @@
             pltpu.VMEM((planes,) + pair, BF16),
             pltpu.VMEM((planes,) + pair, BF16),
             pltpu.VMEM((planes,) + pair, BF16),
-            pltpu.VMEM((planes,) + pair, F32),
             pltpu.VMEM(whole, F32),
             pltpu.VMEM(whole, F32),
-            pltpu.VMEM(features.shape, F32),
+            pltpu.VMEM(features.shape, BF16),
+            pltpu.VMEM(features.shape, BF16),
+            pltpu.VMEM((4, rim, cols, channels), BF16),
             pltpu.VMEM((pixels, channels), F32),
             pltpu.VMEM((pixels, channels), F32),
             pltpu.VMEM((pixels, LANES), F32),
@@ -674,7 +694,7 @@
     )(
         features,
         cotangent,
-        kernel.reshape(tap_total, channels),
+        kernel,
         norm_gain.reshape(1, channels),
         norm_bias.reshape(1, channels),
         in_weight,
@@ -682,17 +702,17 @@
         out_weight,
         layer_scale.reshape(1, channels),
     )
-    output, input_grad, in_weight_grad, out_weight_grad, sums = results
+    output, input_grad, in_weight_grad, out_weight_grad, kernel_grad, sums = results
     return (
         output,
         input_grad,
         in_weight_grad,
         out_weight_grad,
-        sums[:tap_total].reshape(taps, taps, channels),
-        sums[tap_total],
-        sums[tap_total + 1],
-        sums[tap_total + 3 : small_rows].reshape(hidden),
-        sums[tap_total + 2],
+        kernel_grad,
+        sums[0],
+        sums[1],
+        sums[3:].reshape(hidden),
+        sums[2],
     )
 
 

time: 111 us -> 85 us (0.77)
  Pallas kernels: 100 us -> 75.5 us
  local copies, waits for them, and re-layouts: 9.74 us -> 7.49 us
    pallas_call x1, Pallas kernels: 100 us -> 75.5 us  [per_device_fused(): pl.pallas_call(body, out_shape=(jax.ShapeDtypeStruct(features.shape, F32)...]
    reshape x2 -> x0, local copies, waits for them, and re-layouts: 3.16 us -> none  [the longest x1 1.6 us: per_device_fused(): sums[:tap_total].reshape(taps, taps, channels)]
    unnamed x14 -> x17, local copies, waits for them, and re-layouts: 5.16 us -> 6.05 us
where the time goes in v2:
time: 85 us; the launch traced here: 83.7 us
  Pallas kernels  75.5 us (89%)
  local copies, waits for them, and re-layouts  7.49 us (9%)
    pallas_call x1, Pallas kernels, per_device_fused(): pl.pallas_call(body, out_shape=(jax.ShapeDtypeStruct(features.shape, F32)...  75.5 us
    unnamed x17, local copies, waits for them, and re-layouts  6.05 us

profile of v2, /device:TPU:0, one launch (start us, length us, event | category | flops | bytes accessed | tf_op | source)
XLA Modules:
  0.0 83.7 jit_solution(5637160671793419718)
XLA Ops:
  0.6 75.5 %convnext_block.1 = (f32[4,32,512]{2,1,0:T(8,128)}, f32[4,32,512]{2,1,0:T(8,128)}, f32[32,2048]{1,0:T(8,128)}, f32[32,2048]{1,0:T(8,128)}, f32[7,7,512]{2,1,0:T(8,128)}, /*index=5*/f32[7,512]{1,0:T(8,128)}) custom-call(f32[4,32,512]{2,1,0:T(8,128)} %feat.1, f32[4,32,512]{2,1,0:T(8,128)} %cot.1, f32[7,7,512]{2,1,0:T(8,128)} %kern.1, f32[1,512]{1,0:T(1,128)} %bitcast.12, ...), custom_call_target="tpu_custom_call" | custom-call | tf_op jit(solution)/shard_map/convnext_block/pallas_call | solution.py:639
  76.1 0.0 copy-start.4
  76.2 1.4 %fusion = (f32[1,512]{1,0:T(1,128)}, f32[1,512]{1,0:T(1,128)}, f32[1,512]{1,0:T(1,128)}) fusion(f32[7,512]{1,0:T(8,128)} %get-tuple-element.20), kind=kLoop, calls=%fused_computation.1 | loop fusion | bytes 12288 | tf_op jit(solution)/shard_map/slice | solution.py:715
  77.6 0.0 copy-done.4
  77.6 0.6 copy.18
  78.2 0.0 copy-start.2
  78.2 1.7 %copy.24 = f32[4,32,512]{2,1,0:T(8,128)} copy(f32[4,32,512]{2,1,0:T(8,128)} %get-tuple-element.33) | data formatting | bytes 524288
  79.9 0.0 copy-done.2
  79.9 0.0 copy-start.1
  79.9 0.7 copy.25
  80.6 0.3 copy-done.1
  81.0 0.0 copy-start
  81.0 0.7 copy.26
  81.7 0.3 copy-done
  82.0 0.0 copy-start.3
  82.0 0.7 copy.27
  82.7 0.3 copy-done.3
  83.0 0.6 copy.28
  (1 shorter events, 0.0 us)
Async XLA Ops:
  76.1 1.5 %copy-start.4 = (f32[7,512]{1,0:T(8,128)S(1)}, f32[7,512]{1,0:T(8,128)}, u32[]{:S(2)}) copy-start(f32[7,512]{1,0:T(8,128)} %get-tuple-element.20) | copy-start | bytes 43012
  78.2 1.7 %copy-start.2 = (f32[4,32,512]{2,1,0:T(8,128)S(1)}, f32[4,32,512]{2,1,0:T(8,128)}, u32[]{:S(2)}) copy-start(f32[4,32,512]{2,1,0:T(8,128)} %get-tuple-element.34) | copy-start | bytes 786436
  79.9 1.0 %copy-start.1 = (f32[32,2048]{1,0:T(8,128)S(1)}, f32[32,2048]{1,0:T(8,128)}, u32[]{:S(2)}) copy-start(f32[32,2048]{1,0:T(8,128)} %get-tuple-element.35) | copy-start | bytes 786436
  81.0 1.0 %copy-start = (f32[32,2048]{1,0:T(8,128)S(1)}, f32[32,2048]{1,0:T(8,128)}, u32[]{:S(2)}) copy-start(f32[32,2048]{1,0:T(8,128)} %get-tuple-element.36) | copy-start | bytes 786436
  82.0 1.0 %copy-start.3 = (f32[7,7,512]{2,1,0:T(8,128)S(1)}, f32[7,7,512]{2,1,0:T(8,128)}, u32[]{:S(2)}) copy-start(f32[7,7,512]{2,1,0:T(8,128)} %get-tuple-element.37) | copy-start | bytes 301060

commit v3 on v2

--- a/solution.py
+++ b/solution.py
@@ -576,8 +576,8 @@
 
         lax.fori_loop(0, channels // LANES, back_step, 0)
         small_add(1)
+        small_add(2)
         each_of(near_order, pass_on, xpos)
-        small_add(2)
         x_copy(z).wait_recv()
         mine = pair_sum(z, xpos) + from_x[z].astype(F32)
         gw_in[...] = mine[0]

time: 85 us -> 84.7 us (level)
  no operation moved by 1% of the time
where the time goes in v3:
time: 84.7 us; the launch traced here: 83.4 us
  Pallas kernels  75.2 us (89%)
  local copies, waits for them, and re-layouts  7.49 us (9%)
    pallas_call x1, Pallas kernels, per_device_fused(): pl.pallas_call(body, out_shape=(jax.ShapeDtypeStruct(features.shape, F32)...  75.2 us
    unnamed x17, local copies, waits for them, and re-layouts  6.05 us

profile of v3, /device:TPU:0, one launch (start us, length us, event | category | flops | bytes accessed | tf_op | source)
XLA Modules:
  0.0 83.4 jit_solution(13577168314890671811)
XLA Ops:
  0.6 75.2 %convnext_block.1 = (f32[4,32,512]{2,1,0:T(8,128)}, f32[4,32,512]{2,1,0:T(8,128)}, f32[32,2048]{1,0:T(8,128)}, f32[32,2048]{1,0:T(8,128)}, f32[7,7,512]{2,1,0:T(8,128)}, /*index=5*/f32[7,512]{1,0:T(8,128)}) custom-call(f32[4,32,512]{2,1,0:T(8,128)} %feat.1, f32[4,32,512]{2,1,0:T(8,128)} %cot.1, f32[7,7,512]{2,1,0:T(8,128)} %kern.1, f32[1,512]{1,0:T(1,128)} %bitcast.12, ...), custom_call_target="tpu_custom_call" | custom-call | tf_op jit(solution)/shard_map/convnext_block/pallas_call | solution.py:639
  75.9 0.0 copy-start.4
  75.9 1.4 %fusion = (f32[1,512]{1,0:T(1,128)}, f32[1,512]{1,0:T(1,128)}, f32[1,512]{1,0:T(1,128)}) fusion(f32[7,512]{1,0:T(8,128)} %get-tuple-element.20), kind=kLoop, calls=%fused_computation.1 | loop fusion | bytes 12288 | tf_op jit(solution)/shard_map/slice | solution.py:715
  77.4 0.0 copy-done.4
  77.4 0.6 copy.18
  78.0 0.0 copy-start.2
  78.0 1.7 %copy.24 = f32[4,32,512]{2,1,0:T(8,128)} copy(f32[4,32,512]{2,1,0:T(8,128)} %get-tuple-element.33) | data formatting | bytes 524288
  79.7 0.0 copy-done.2
  79.7 0.0 copy-start.1
  79.7 0.7 copy.25
  80.4 0.3 copy-done.1
  80.7 0.0 copy-start
  80.7 0.7 copy.26
  81.4 0.3 copy-done
  81.8 0.0 copy-start.3
  81.8 0.7 copy.27
  82.5 0.3 copy-done.3
  82.8 0.6 copy.28
  (1 shorter events, 0.0 us)
Async XLA Ops:
  75.9 1.5 %copy-start.4 = (f32[7,512]{1,0:T(8,128)S(1)}, f32[7,512]{1,0:T(8,128)}, u32[]{:S(2)}) copy-start(f32[7,512]{1,0:T(8,128)} %get-tuple-element.20) | copy-start | bytes 43012
  78.0 1.7 %copy-start.2 = (f32[4,32,512]{2,1,0:T(8,128)S(1)}, f32[4,32,512]{2,1,0:T(8,128)}, u32[]{:S(2)}) copy-start(f32[4,32,512]{2,1,0:T(8,128)} %get-tuple-element.34) | copy-start | bytes 786436
  79.7 1.0 %copy-start.1 = (f32[32,2048]{1,0:T(8,128)S(1)}, f32[32,2048]{1,0:T(8,128)}, u32[]{:S(2)}) copy-start(f32[32,2048]{1,0:T(8,128)} %get-tuple-element.35) | copy-start | bytes 786436
  80.7 1.0 %copy-start = (f32[32,2048]{1,0:T(8,128)S(1)}, f32[32,2048]{1,0:T(8,128)}, u32[]{:S(2)}) copy-start(f32[32,2048]{1,0:T(8,128)} %get-tuple-element.36) | copy-start | bytes 786436
  81.8 1.0 %copy-start.3 = (f32[7,7,512]{2,1,0:T(8,128)S(1)}, f32[7,7,512]{2,1,0:T(8,128)}, u32[]{:S(2)}) copy-start(f32[7,7,512]{2,1,0:T(8,128)} %get-tuple-element.37) | copy-start | bytes 301060
